TPU v7x, 32 devices: a whole 2x2x4 slice. The times are simulated.
32 devices in a mesh: parts: 2 (over y), patch: 4 (over z), level: 2 (over x), sub: 2 (over core).
Axes of the slice: x: 2, y: 2, z: 4, core: 2. Of those that a mesh axis runs over, the one named last changes fastest.
Arguments:
- adjoint_height: float32 [4, 1024, 1024], P(('parts', 'level'), ('patch', 'sub')), parts along dimension 0, may hold values from -6 to 6
- adjoint_momenta: float32 [2, 4, 1024, 1024], P(None, ('parts', 'level'), ('patch', 'sub')), parts along dimension 1, may hold values from -6 to 6
- depth: float32 [2, 1024, 1024], P('level', ('patch', 'sub')), may hold values from 0.2 to 1
- wet_mask: int32 [2, 1024, 1024], P('level', ('patch', 'sub')), may hold values 0 or 1
- adjacency: int32 [2, 4, 4], P('level'), may hold values from -1 to 3, as said below
- nest_gain: float32 [2, 8192], P(None, ('patch', 'sub')), may hold values from 0.75 to 1
- nest_index: int32 [2, 8192], P(None, ('patch', 'sub')), may hold values from 0 to 1023, as said below
Outputs:
- height_out: float32 [4, 1024, 1024], P(('parts', 'level'), ('patch', 'sub')), parts along dimension 0
- momenta_out: float32 [2, 4, 1024, 1024], P(None, ('parts', 'level'), ('patch', 'sub')), parts along dimension 1
There are 2 independent parts, one for each index of `parts`. A program takes and returns all parts, laid end to end along the dimension named above; an argument that names none is the same for every part. Nothing has to cross between parts.
Inputs may be any that keep to these rules, and one draw needn't show every extreme that they name: `adjacency`: the patches of a level sit on a grid of cells in an order drawn from the seed; each row of a patch lists its grid neighbours, -1 at the grid's edge, and neighbour links are symmetric. `nest_index`: entries index a cell of the same half patch's strip, 1024 cells long.
All inputs are finite; a program needn't handle non-finite values. No bound on the sum of `wet_mask` on one device may be relied on, other than what follows from the above.
Results may differ from a plain program's by a relative error of at most 0.00002.
Values sent between devices are 32-bit elements; how exact they have to be, the bound alone decides.
A program may use at most 64 MiB of HBM per device.

v0:
```python
import jax
import jax.numpy as jnp
from jax import lax
from jax.sharding import PartitionSpec as P

STEPS = 2


courant = 0.45


def passed_along(value, axis, steps):
    count = lax.axis_size(axis)
    initial, last = (max(0, -steps), min(count, count - steps))
    return lax.ppermute(value, axis, [(source, source + steps) for source in range(initial, last)])


def pick_row(table, index):
    return lax.dynamic_index_in_dim(table, index, 0, keepdims=False)


def body(adjoint_height, adjoint_momenta, depth, wet_mask, adjacency, nest_gain, nest_index):
    eta = adjoint_height[0]
    mom_row = adjoint_momenta[0, 0]
    mom_col = adjoint_momenta[1, 0]
    height = depth[0]
    wet = wet_mask[0].astype(jnp.float32)
    level = lax.axis_index("level")
    patch = lax.axis_index("patch")
    half = lax.axis_index("sub")
    levels = lax.axis_size("level")
    subs = lax.axis_size("sub")
    segments = lax.axis_size("patch") * subs
    links = pick_row(adjacency[0], patch)
    north = links[0]
    south = links[1]
    west = links[2]
    east = links[3]
    has_north = (north >= 0).astype(jnp.float32)
    has_south = (south >= 0).astype(jnp.float32)
    has_west = (west >= 0).astype(jnp.float32)
    has_east = (east >= 0).astype(jnp.float32)
    own_gain = pick_row(nest_gain, level)
    own_table = pick_row(nest_index, level)
    for step in range(STEPS):
        strip = eta[0]
        flux = strip
        inflow = jnp.zeros_like(strip)
        for turn in range(levels - 1):
            received = passed_along(flux, "level", -1)
            inflow = own_gain * jnp.take(received, own_table)
            flux = inflow + strip
        eta = eta.at[0].add(inflow)
        first_col = eta[:, 0]
        first_row = eta[0, :]
        east_cols = lax.all_gather(first_col[None], ("patch", "sub"), axis=0, tiled=True)
        east_rows = lax.all_gather(first_row[None], ("patch", "sub"), axis=0, tiled=True)
        east_col = jnp.take(east_cols, jnp.maximum(east, 0) * subs + half, axis=0) * has_east
        east_inside = jnp.take(
            east_rows, jnp.minimum(patch * subs + half + 1, segments - 1), axis=0
        )
        east_across = jnp.take(east_rows, jnp.maximum(south, 0) * subs, axis=0) * has_south
        south_row = jnp.where(half == subs - 1, east_across, east_inside)
        east_col, south_row = (east_col, south_row)
        east_eta = jnp.concatenate([eta[:, 1:], east_col[:, None]], axis=1)
        south_eta = jnp.concatenate([eta[1:], south_row[None]], axis=0)
        mom_row = wet * (mom_row - courant * (east_eta - eta))
        mom_col = wet * (mom_col - courant * (south_eta - eta))
        last_col = mom_row[:, -1]
        last_row = mom_col[-1, :]
        cols = lax.all_gather(last_col[None], ("patch", "sub"), axis=0, tiled=True)
        rows = lax.all_gather(last_row[None], ("patch", "sub"), axis=0, tiled=True)
        west_col = jnp.take(cols, jnp.maximum(west, 0) * subs + half, axis=0) * has_west
        inside = jnp.take(rows, jnp.maximum(patch * subs + half - 1, 0), axis=0)
        across = jnp.take(rows, jnp.maximum(north, 0) * subs + subs - 1, axis=0) * has_north
        north_row = jnp.where(half == 0, across, inside)
        west_col, north_row = (west_col, north_row)
        west_row = jnp.concatenate([west_col[:, None], mom_row[:, :-1]], axis=1)
        north_col = jnp.concatenate([north_row[None], mom_col[:-1]], axis=0)
        eta = wet * (eta - courant * height * (mom_row - west_row + (mom_col - north_col)))
    return (eta[None], jnp.stack([mom_row, mom_col])[:, None])


def solution(mesh):
    in_specs = (
        P(("parts", "level"), ("patch", "sub"), None),
        P(None, ("parts", "level"), ("patch", "sub"), None),
        P("level", ("patch", "sub"), None),
        P("level", ("patch", "sub"), None),
        P("level", None, None),
        P(None, ("patch", "sub")),
        P(None, ("patch", "sub")),
    )
    out_specs = (
        P(("parts", "level"), ("patch", "sub"), None),
        P(None, ("parts", "level"), ("patch", "sub"), None),
    )
    return jax.shard_map(body, mesh=mesh, in_specs=in_specs, out_specs=out_specs, check_vma=False)
```

profile of v0, /device:TPU:0, one launch (start us, length us, event | category | flops | bytes accessed | tf_op | source)
XLA Modules:
  0.0 152.6 jit_solution(2689515999720986161)
XLA Ops:
  0.6 0.0 copy-start
  0.6 1.0 copy.33
  1.7 1.3 collective-permute-start
  3.0 0.7 constant_dynamic-slice_fusion.4
  3.7 0.6 fusion.35
  4.3 0.0 copy-done
  4.3 0.0 copy-start.4
  4.3 0.7 copy-done.4
  10.1 0.0 collective-permute-done
  10.2 4.5 %gather_fusion = f32[1024]{0:T(1024)S(1)} fusion(f32[1024]{0:T(1024)S(1)} %collective-permute-done, s32[1024]{0:T(1024)S(1)} %fusion.22), kind=kCustom, calls=%fused_computation.clone | custom fusion | bytes 12288 | tf_op jit(solution)/shard_map/jit(_take)/gather | solution.py:51
  14.7 15.7 %all-gather.2 = f32[8192]{0:T(1024)S(1)} all-gather(f32[1024]{0:T(1024)S(1)} %get-tuple-element.51), channel_id=4, replica_groups=mesh['parts'=2,'patch'=4,'level'=2,'sub'=2] {'patch','sub'}, dimensions={0}, use_global_device_ids=true | all-gather | bytes 36864 | tf_op jit(solution)/shard_map/all_gather | solution.py:57
  30.4 0.1 scatter-add.6
  30.5 0.2 slice.143
  30.7 0.0 copy-start.1
  30.8 14.8 %all-gather = f32[1024,1]{1,0:T(8,128)S(1)} all-gather(f32[128,1]{1,0:T(8,128)S(1)} %slice.144), channel_id=2, replica_groups=mesh['parts'=2,'patch'=4,'level'=2,'sub'=2] {'patch','sub'}, dimensions={0}, use_global_device_ids=true | all-gather | bytes 4608 | tf_op jit(solution)/shard_map/all_gather | solution.py:56
  45.6 0.2 reduce.4
  45.8 0.1 copy.17
  46.0 0.0 copy-done.1
  46.0 1.6 %fusion.9 = (f32[128,1024]{1,0:T(8,128)S(1)}, f32[128,1024]{1,0:T(8,128)S(1)}) fusion(f32[128,1024]{1,0:T(8,128)S(1)} %scatter-add.6, f32[1,1024]{1,0:T(1,128)S(1)} %bitcast.119, f32[127,1024]{1,0:T(8,128)S(1)} %slice.147, f32[2,1,128,1024]{3,2,1,0:T(8,128)} %param.18, s32[1,128,1024]{2,1,0:T(8,128)S(1)} %copy-done.1, f32[128,1]{1,0:T(8,128)S(1)} %copy.17, ...), kind=kLoop, calls=%fused_computation.15 | loop fusion | flops 1441792 | bytes 4194304 | tf_op jit(solution)/shard_map/mul | solution.py:68
  47.6 14.2 %all-gather.5 = f32[8,1,1024]{2,1,0:T(1,128)S(1)} all-gather(f32[1,1,1024]{2,1,0:T(1,128)S(1)} %slice_bitcast_fusion.1), channel_id=1, replica_groups=mesh['parts'=2,'patch'=4,'level'=2,'sub'=2] {'patch','sub'}, dimensions={0}, use_global_device_ids=true | all-gather | bytes 36864 | tf_op jit(solution)/shard_map/all_gather | solution.py:72
  61.8 0.1 slice.145
  61.9 0.0 copy-start.2
  61.9 15.0 %all-gather.1 = f32[1024,1]{1,0:T(8,128)S(1)} all-gather(f32[128,1]{1,0:T(8,128)S(1)} %slice.145), channel_id=3, replica_groups=mesh['parts'=2,'patch'=4,'level'=2,'sub'=2] {'patch','sub'}, dimensions={0}, use_global_device_ids=true | all-gather | bytes 4608 | tf_op jit(solution)/shard_map/all_gather | solution.py:71
  76.9 0.2 reduce.5
  77.2 0.1 copy.18
  77.3 0.0 copy-done.2
  77.3 0.4 fusion.6
  77.7 1.3 collective-permute-start.1
  79.0 4.2 %collective-permute-done.1 = f32[1024]{0:T(1024)S(1)} collective-permute-done((f32[1024]{0:T(1024)S(1)}, f32[1024]{0:T(1024)S(1)}, u32[]{:S(2)}, u32[]{:S(2)}) %collective-permute-start.1) | collective-permute-done | bytes 4128 | tf_op jit(solution)/shard_map/ppermute | solution.py:15
  83.2 4.5 %gather_fusion.1 = f32[1024]{0:T(1024)S(1)} fusion(f32[1024]{0:T(1024)S(1)} %collective-permute-done.1, s32[1024]{0:T(1024)S(1)} %fusion.22), kind=kCustom, calls=%fused_computation.1.clone | custom fusion | bytes 12288 | tf_op jit(solution)/shard_map/jit(_take)/gather | solution.py:51
  87.8 0.1 scatter-add.9
  87.9 0.8 slice.155
  88.8 1.0 slice.151
  89.8 14.0 %all-gather.6 = f32[8,1,1024]{2,1,0:T(1,128)S(1)} all-gather(f32[1,1,1024]{2,1,0:T(1,128)S(1)} %bitcast.111), channel_id=1, replica_groups=mesh['parts'=2,'patch'=4,'level'=2,'sub'=2] {'patch','sub'}, dimensions={0}, use_global_device_ids=true | all-gather | bytes 36864 | tf_op jit(solution)/shard_map/all_gather | solution.py:57
  103.8 14.9 %all-gather.3 = f32[1024,1]{1,0:T(8,128)S(1)} all-gather(f32[128,1]{1,0:T(8,128)S(1)} %slice.152), channel_id=5, replica_groups=mesh['parts'=2,'patch'=4,'level'=2,'sub'=2] {'patch','sub'}, dimensions={0}, use_global_device_ids=true | all-gather | bytes 4608 | tf_op jit(solution)/shard_map/all_gather | solution.py:56
  118.7 0.2 reduce.6
  118.9 0.1 copy.19
  119.1 1.6 %fusion.20 = (f32[128,1024]{1,0:T(8,128)S(1)}, f32[128,1024]{1,0:T(8,128)S(1)}) fusion(f32[128,1024]{1,0:T(8,128)S(1)} %get-tuple-element.53, f32[128,1024]{1,0:T(8,128)S(1)} %scatter-add.9, f32[1,1024]{1,0:T(1,128)S(1)} %bitcast.117, f32[127,1024]{1,0:T(8,128)} %slice.155, s32[1,128,1024]{2,1,0:T(8,128)S(1)} %copy-done.1, ...), kind=kLoop, calls=%fused_computation.30 | loop fusion | flops 1441792 | bytes 4194304 | tf_op jit(solution)/shard_map/mul | solution.py:68
  120.6 14.3 %all-gather.7 = f32[8,1,1024]{2,1,0:T(1,128)S(1)} all-gather(f32[1,1,1024]{2,1,0:T(1,128)S(1)} %slice_bitcast_fusion), channel_id=1, replica_groups=mesh['parts'=2,'patch'=4,'level'=2,'sub'=2] {'patch','sub'}, dimensions={0}, use_global_device_ids=true | all-gather | bytes 36864 | tf_op jit(solution)/shard_map/all_gather | solution.py:72
  134.9 0.1 slice.153
  135.0 14.9 %all-gather.4 = f32[1024,1]{1,0:T(8,128)S(1)} all-gather(f32[128,1]{1,0:T(8,128)S(1)} %slice.153), channel_id=6, replica_groups=mesh['parts'=2,'patch'=4,'level'=2,'sub'=2] {'patch','sub'}, dimensions={0}, use_global_device_ids=true | all-gather | bytes 4608 | tf_op jit(solution)/shard_map/all_gather | solution.py:71
  149.9 0.2 reduce.7
  150.1 0.1 copy.20
  150.2 0.0 copy-start.3
  150.3 1.1 maximum_bitcast_fusion
  151.3 0.1 copy-done.3
  151.4 1.2 fusion.17
  (29 shorter events, 0.3 us)
Async XLA Ops:
  0.6 3.7 %copy-start = (s32[2,1024]{1,0:T(2,128)S(1)}, s32[2,1024]{1,0:T(2,128)}, u32[]{:S(2)}) copy-start(s32[2,1024]{1,0:T(2,128)} %param.23) | copy-start | bytes 24580
  1.7 8.4 %collective-permute-start = (f32[1024]{0:T(1024)S(1)}, f32[1024]{0:T(1024)S(1)}, u32[]{:S(2)}, u32[]{:S(2)}) collective-permute-start(f32[1024]{0:T(1024)S(1)} %bitcast.122), channel_id=1, source_target_pairs={{2,0},{3,1},{6,4},{7,5},{10,8},{11,9},{14,12},{15,13},{18,16},{19,... | collective-permute-start | bytes 12296 | tf_op jit(solution)/shard_map/ppermute | solution.py:15
  4.3 0.7 copy-start.4
  30.7 15.2 %copy-start.1 = (s32[1,128,1024]{2,1,0:T(8,128)S(1)}, s32[1,128,1024]{2,1,0:T(8,128)}, u32[]{:S(2)}) copy-start(s32[1,128,1024]{2,1,0:T(8,128)} %param.20) | copy-start | bytes 1572868
  61.9 15.4 %copy-start.2 = (f32[1,128,1024]{2,1,0:T(8,128)S(1)}, f32[1,128,1024]{2,1,0:T(8,128)}, u32[]{:S(2)}) copy-start(f32[1,128,1024]{2,1,0:T(8,128)} %param.19) | copy-start | bytes 1572868
  77.7 5.5 %collective-permute-start.1 = (f32[1024]{0:T(1024)S(1)}, f32[1024]{0:T(1024)S(1)}, u32[]{:S(2)}, u32[]{:S(2)}) collective-permute-start(f32[1024]{0:T(1024)S(1)} %bitcast.136), channel_id=1, source_target_pairs={{2,0},{3,1},{6,4},{7,5},{10,8},{11,9},{14,12},{15,13},{18,16},{19,... | collective-permute-start | bytes 12296 | tf_op jit(solution)/shard_map/ppermute | solution.py:15
  150.2 1.1 copy-start.3
where the time goes:
time: 153 us
  blocking collectives  118 us (77%)
  local copies, waits for them, and re-layouts  15.1 us (10%)
  other arithmetic  6.77 us (4%)
  between operations  6.05 us (4%)
  waiting for transfers between devices  4.2 us (3%)
  starting transfers between devices  2.57 us (2%)
    all_gather x2, blocking collectives, body(): cols = lax.all_gather(last_col[None], ('patch', 'sub'), axis=0, tiled=True)  29.9 us
    all_gather x2, blocking collectives, body(): lax.all_gather(first_col[None], ('patch', 'sub'), axis=0, tiled=True)  29.8 us
    all_gather x2, blocking collectives, body(): lax.all_gather(first_row[None], ('patch', 'sub'), axis=0, tiled=True)  29.7 us
    all_gather x2, blocking collectives, body(): rows = lax.all_gather(last_row[None], ('patch', 'sub'), axis=0, tiled=True)  28.5 us
    gather x2, local copies, waits for them, and re-layouts, body(): inflow = own_gain * jnp.take(received, own_table)  9.05 us
    ppermute x2, waiting for transfers between devices, passed_along(): lax.ppermute(value, axis, [(source, source + steps) for source in range(i...  4.2 us
    mul x2, other arithmetic, body(): mom_col = wet * (mom_col - courant * (south_eta - eta))  3.13 us
  transfers between devices with their start and end apart: 2, of which 1 were waited for; matrix products, arithmetic and copies ran while one was open for 1% of the time, Pallas kernels for 0%

commit v1 on v0

v1 whole, which is shorter than its diff:
```python
import functools

import jax
import jax.numpy as jnp
from jax import lax
from jax.experimental import pallas as pl
from jax.experimental.pallas import tpu as pltpu
from jax.sharding import PartitionSpec as P

STEPS = 2
COURANT = 0.45
LANES = 128
BLOCK = 8


def kernel(patches, levels, rows, cols,
           adj, eta_hbm, mom_hbm, depth_hbm, wet_hbm, gain_hbm, table_hbm,
           eta_out, mom_out,
           E, Pm, Q, H, W, gain_v, table_v, f8, idx8, gain8, tmp,
           sfirst, slast, scol, sinf, sew,
           rown, in_sems, out_sems, send_sems, recv_sems, own_sems, *landing):
    rfirst, rlast, rcol, rnbr, rew = (landing[n * STEPS:(n + 1) * STEPS] for n in range(5))
    patch = lax.axis_index("patch")
    level = lax.axis_index("level")
    half = lax.axis_index("sub")
    chunks = cols // LANES
    other = 1 - half

    loads = [
        pltpu.make_async_copy(eta_hbm.at[0], E.at[0:rows], in_sems.at[0]),
        pltpu.make_async_copy(mom_hbm.at[0, 0], Pm, in_sems.at[1]),
        pltpu.make_async_copy(mom_hbm.at[1, 0], Q.at[8:8 + rows], in_sems.at[2]),
        pltpu.make_async_copy(wet_hbm.at[0], W, in_sems.at[3]),
        pltpu.make_async_copy(table_hbm, table_v, in_sems.at[4]),
        pltpu.make_async_copy(gain_hbm, gain_v, in_sems.at[5]),
        pltpu.make_async_copy(depth_hbm.at[0], H, in_sems.at[6]),
    ]
    for load in loads:
        load.start()

    barrier = pltpu.get_barrier_semaphore()

    def greet(d, h, lev):
        pl.semaphore_signal(barrier, inc=1, device_id={
            "patch": lax.rem(patch + d, patches), "sub": h, "level": lev},
            device_id_type=pl.DeviceIdType.MESH)

    for d in range(patches):
        if d:
            greet(d, half, level)
        greet(d, other, level)

    @pl.when(level > 0)
    def _():
        for d in range(patches):
            greet(d, half, level - 1)
            greet(d, other, level - 1)

    @pl.when(level < levels - 1)
    def _():
        for d in range(patches):
            greet(d, half, level + 1)
            greet(d, other, level + 1)

    sides = (level > 0).astype(jnp.int32) + (level < levels - 1).astype(jnp.int32)
    pl.semaphore_wait(barrier, 2 * patches - 1 + 2 * patches * sides)

    for load in loads[:6]:
        load.wait()

    lower = jnp.maximum(level - 1, 0)
    for c in range(chunks):
        lane = slice(c * LANES, (c + 1) * LANES)
        index, gain = table_v[0:1, lane], gain_v[0:1, lane]
        for lev in range(1, levels - 1):
            index = jnp.where(lower == lev, table_v[lev:lev + 1, lane], index)
            gain = jnp.where(lower == lev, gain_v[lev:lev + 1, lane], gain)
        idx8[c:c + 1, :] = index
        gain8[c:c + 1, :] = gain

    def remote(t, kind, src, buf, slot, d, h, lev):
        return pltpu.make_async_remote_copy(
            src_ref=src, dst_ref=buf, send_sem=send_sems.at[t, kind, d],
            recv_sem=recv_sems.at[t, kind, slot],
            device_id={"patch": lax.rem(patch + d, patches), "sub": h, "level": lev},
            device_id_type=pl.DeviceIdType.MESH)

    def slot_of(d):
        return lax.rem(patch + d, patches)

    def last_part(t):
        return slice(0, 2) if t == 0 else slice(t + 1, t + 2)

    def halo_copies(t, slot, d):
        col = remote(t, 0, scol.at[t], rcol[t].at[slot], slot, d, half, level)
        first = remote(t, 1, sfirst.at[t], rfirst[t].at[slot], slot, d, other, level)
        part = last_part(t)
        last = remote(t, 2, slast.at[part], rlast[t].at[slot], slot, d, other, level)
        return col, first, last

    def inf_copies(t, slot, d):
        beside = remote(t, 3, sinf.at[t], rnbr[t].at[slot], slot, d, other, lower)
        ends = remote(t, 4, sew.at[t], rew[t].at[slot], slot, d, half, lower)
        return beside, ends

    def own_copy(t):
        return pltpu.make_async_remote_copy(
            src_ref=sinf.at[t], dst_ref=rown.at[t], send_sem=own_sems.at[t, 0],
            recv_sem=own_sems.at[t, 1], device_id={"level": lower},
            device_id_type=pl.DeviceIdType.MESH)

    def send_inflow(t):
        for c in range(chunks):
            f8[c:c + 1, :] = E[0:1, c * LANES:(c + 1) * LANES]
        index = idx8[...]
        inside = jnp.bitwise_and(index, LANES - 1)
        which = lax.shift_right_logical(index, 7)
        picked = jnp.zeros((chunks, LANES), jnp.float32)
        for c in range(chunks):
            source = jnp.broadcast_to(f8[c:c + 1, :], (chunks, LANES))
            got = jnp.take_along_axis(source, inside, axis=1, mode="promise_in_bounds")
            picked = jnp.where(which == c, got, picked)
        inflow = gain8[...] * picked
        sinf[t] = inflow
        own_copy(t).start()
        sew[t, 0:1, :] = inflow[0:1, :]
        sew[t, 1:2, :] = pltpu.roll(inflow[chunks - 1:chunks, :], 1, 1)
        for d in range(patches):
            beside, ends = inf_copies(t, patch, d)

            @pl.when(half == (1 if d == 0 else 0))
            def _():
                beside.start()
            if d:
                ends.start()

    def inflow_waits(t):
        for d in range(patches):
            beside, ends = inf_copies(t, slot_of(d), d)

            @pl.when(half == (0 if d == 0 else 1))
            def _():
                beside.wait_recv()
            if d:
                ends.wait_recv()

    def inflow_send_waits(t):
        own_copy(t).wait_send()
        for d in range(patches):
            beside, ends = inf_copies(t, patch, d)

            @pl.when(half == (1 if d == 0 else 0))
            def _():
                beside.wait_send()
            if d:
                ends.wait_send()

    def each_halo(t, first_when, last_when, act, sending):
        for d in range(patches):
            col, first, last = halo_copies(t, patch if sending else slot_of(d), d)

            @pl.when(half == (first_when if d == 0 else 1 - first_when))
            def _():
                act(first)

            @pl.when(half == (last_when if d == 0 else 1 - last_when))
            def _():
                act(last)
            if d:
                act(col)

    north = adj[0, patch, 0]
    south = adj[0, patch, 1]
    west = adj[0, patch, 2]
    east = adj[0, patch, 3]
    south_ok = jnp.logical_or(half == 0, south >= 0)
    north_ok = jnp.logical_or(half == 1, north >= 0)
    south_at = jnp.where(half == 0, patch, jnp.maximum(south, 0))
    north_at = jnp.where(half == 1, patch, jnp.maximum(north, 0))
    west_at = jnp.maximum(west, 0)
    east_at = jnp.maximum(east, 0)
    finer = level < levels - 1
    lane_ids = lax.broadcasted_iota(jnp.int32, (rows, LANES), 1)
    first_lane = lax.broadcasted_iota(jnp.int32, (1, LANES), 1) == 0
    wide_ids = lax.broadcasted_iota(jnp.int32, (BLOCK, cols), 1)
    tail = slice(cols - LANES, cols)
    end = rows - 1

    for t in range(STEPS):
        @pl.when(level == levels - 1)
        def _():
            send_inflow(t)

        sfirst[t] = E[0:1, :]
        wet_row = W[end:rows, :].astype(jnp.float32)
        slast[t + 1] = wet_row * (Q[8 + end:8 + rows, :] + COURANT * E[end:rows, :])
        if t == 0:
            slast[0] = wet_row
        wet_tail = W[:, tail].astype(jnp.float32)
        share = wet_tail * (Pm[:, tail] + COURANT * E[0:rows, tail])
        mixed = jnp.where(lane_ids == 0, E[0:rows, 0:LANES],
                          jnp.where(lane_ids == 1, pltpu.roll(share, 2, 1),
                                    pltpu.roll(wet_tail, 3, 1)))
        scol[t] = jnp.transpose(mixed)[0:8, :]
        each_halo(t, 1, 0, lambda copy: copy.start(), True)

        @pl.when(finer)
        def _():
            own_copy(t).wait_recv()
            for c in range(chunks):
                lane = slice(c * LANES, (c + 1) * LANES)
                E[0:1, lane] += rown[t, c:c + 1, :]

        if levels > 2:
            @pl.when(jnp.logical_and(level > 0, level < levels - 1))
            def _():
                send_inflow(t)

        each_halo(t, 0, 1, lambda copy: copy.wait_recv(), False)

        @pl.when(finer)
        def _():
            inflow_waits(t)

        east_row = rcol[t][east_at][0:1, :]
        east_row += jnp.where(jnp.logical_and(first_lane, finer), rew[t][east_at][0:1, :], 0.0)
        west_cols = rcol[t][west_at]
        share = west_cols[1:2, :]
        wet_w = west_cols[2:3, :]
        share += jnp.where(jnp.logical_and(first_lane, finer),
                           COURANT * wet_w * rew[t][west_at][1:2, :], 0.0)
        tmp[0:1, :] = jnp.where(east >= 0, east_row, 0.0)
        tmp[1:2, :] = jnp.where(west >= 0, share, 0.0)
        tmp[2:3, :] = jnp.where(west >= 0, wet_w, 0.0)
        halo = jnp.transpose(tmp[...])
        beside = rnbr[t][south_at]
        below = rfirst[t][south_at]
        for c in range(chunks):
            lane = slice(c * LANES, (c + 1) * LANES)
            value = below[:, lane] + jnp.where(finer, beside[c:c + 1, :], 0.0)
            E[rows:rows + 1, lane] = jnp.where(south_ok, value, 0.0)
        share_n = rlast[t][north_at, 1 if t == 0 else 0]
        wet_n = rlast[0][north_at, 0]
        Q[7:8, :] = jnp.where(north_ok, share_n - COURANT * wet_n * E[0:1, :], 0.0)
        if t == 0:
            loads[6].wait()

        for r in range(0, rows, BLOCK):
            span = slice(r, r + BLOCK)
            e = E[span, :]
            wet = W[span, :].astype(jnp.float32)
            e_south = E[r + 1:r + 1 + BLOCK, :]
            e_east = jnp.where(wide_ids == cols - 1, halo[span, 0:1], pltpu.roll(e, cols - 1, 1))
            p = wet * (Pm[span, :] - COURANT * (e_east - e))
            q = wet * (Q[8 + r:16 + r, :] - COURANT * (e_south - e))
            p_edge = halo[span, 1:2] - COURANT * halo[span, 2:3] * e[:, 0:1]
            p_west = jnp.where(wide_ids == 0, p_edge, pltpu.roll(p, 1, 1))
            Pm[span, :] = p
            Q[8 + r:16 + r, :] = q
            q_north = Q[7 + r:15 + r, :]
            E[span, :] = wet * (e - COURANT * H[span, :] * ((p - p_west) + (q - q_north)))

    stores = [
        pltpu.make_async_copy(E.at[0:rows], eta_out.at[0], out_sems.at[0]),
        pltpu.make_async_copy(Pm, mom_out.at[0, 0], out_sems.at[1]),
        pltpu.make_async_copy(Q.at[8:8 + rows], mom_out.at[1, 0], out_sems.at[2]),
    ]
    for store in stores:
        store.start()
    for t in range(STEPS):
        each_halo(t, 1, 0, lambda copy: copy.wait_send(), True)

        @pl.when(level > 0)
        def _():
            inflow_send_waits(t)
    for store in stores:
        store.wait()


def body(mesh, adjoint_height, adjoint_momenta, depth, wet_mask, adjacency, nest_gain, nest_index):
    patches, levels = mesh.shape["patch"], mesh.shape["level"]
    rows, cols = adjoint_height.shape[1:]
    chunks = cols // LANES
    f32 = jnp.float32
    anywhere = pl.BlockSpec(memory_space=pl.ANY)
    v = pltpu.VMEM
    scratch = [
        v((rows + 8, cols), f32), v((rows, cols), f32), v((rows + 8, cols), f32),
        v((rows, cols), f32), v((rows, cols), jnp.int32),
        v(nest_gain.shape, f32), v(nest_index.shape, jnp.int32),
        v((chunks, LANES), f32), v((chunks, LANES), jnp.int32), v((chunks, LANES), f32),
        v((8, LANES), f32),
        v((STEPS, 1, cols), f32), v((STEPS + 1, 1, cols), f32), v((STEPS, 8, LANES), f32),
        v((STEPS, chunks, LANES), f32), v((STEPS, 2, LANES), f32),
        v((STEPS, chunks, LANES), f32),
        pltpu.SemaphoreType.DMA((7,)), pltpu.SemaphoreType.DMA((3,)),
        pltpu.SemaphoreType.DMA((STEPS, 5, patches)), pltpu.SemaphoreType.DMA((STEPS, 5, patches)),
        pltpu.SemaphoreType.DMA((STEPS, 2)),
    ]
    scratch += [v((patches, 1, cols), f32)] * STEPS
    scratch += [v((patches, 2 if t == 0 else 1, 1, cols), f32) for t in range(STEPS)]
    scratch += [v((patches, 8, LANES), f32)] * STEPS
    scratch += [v((patches, chunks, LANES), f32)] * STEPS
    scratch += [v((patches, 2, LANES), f32)] * STEPS
    return pl.pallas_call(
        functools.partial(kernel, patches, levels, rows, cols),
        out_shape=(jax.ShapeDtypeStruct(adjoint_height.shape, f32),
                   jax.ShapeDtypeStruct(adjoint_momenta.shape, f32)),
        in_specs=[pl.BlockSpec(memory_space=pltpu.SMEM)] + [anywhere] * 6,
        out_specs=(anywhere, anywhere),
        scratch_shapes=scratch,
        compiler_params=pltpu.CompilerParams(collective_id=0, has_side_effects=True),
    )(adjacency, adjoint_height, adjoint_momenta, depth, wet_mask, nest_gain, nest_index)


def solution(mesh):
    in_specs = (
        P(("parts", "level"), ("patch", "sub"), None),
        P(None, ("parts", "level"), ("patch", "sub"), None),
        P("level", ("patch", "sub"), None),
        P("level", ("patch", "sub"), None),
        P("level", None, None),
        P(None, ("patch", "sub")),
        P(None, ("patch", "sub")),
    )
    out_specs = (
        P(("parts", "level"), ("patch", "sub"), None),
        P(None, ("parts", "level"), ("patch", "sub"), None),
    )
    return jax.shard_map(functools.partial(body, mesh), mesh=mesh, in_specs=in_specs,
                         out_specs=out_specs, check_vma=False)
```

time: 153 us -> 22.9 us (0.15)
  blocking collectives: 118 us -> 0 us
  Pallas kernels: 0 us -> 19.1 us
  local copies, waits for them, and re-layouts: 15.1 us -> 2.95 us
  other arithmetic: 6.77 us -> 0 us
  between operations: 6.05 us -> 0.65 us
  waiting for transfers between devices: 4.2 us -> 0 us
  starting transfers between devices: 2.57 us -> 0 us
    all_gather x8 -> x0, blocking collectives: 118 us -> none  [the longest x2 29.9 us: body(): cols = lax.all_gather(last_col[None], ('patch', 'sub'), axis=0, tiled=True)]
    pallas_call x0 -> x1, Pallas kernels: none -> 19.1 us  [body(): pl.pallas_call(functools.partial(kernel, patches, levels, rows, cols), ou...]
    gather x2 -> x0, local copies, waits for them, and re-layouts: 9.05 us -> none  [body(): inflow = own_gain * jnp.take(received, own_table)]
    ppermute x2 -> x0, waiting for transfers between devices: 4.2 us -> none  [passed_along(): lax.ppermute(value, axis, [(source, source + steps) for source in range(i...]
    mul x4 -> x0, other arithmetic: 3.54 us -> none  [the longest x2 3.13 us: body(): mom_col = wet * (mom_col - courant * (south_eta - eta))]
    slice x9 -> x0, local copies, waits for them, and re-layouts: 2.88 us -> none  [the longest x2 1.2 us: body(): east_eta = jnp.concatenate([eta[:, 1:], east_col[:, None]], axis=1)]
    ppermute x2 -> x0, starting transfers between devices: 2.57 us -> none  [passed_along(): lax.ppermute(value, axis, [(source, source + steps) for source in range(i...]
    broadcast_in_dim x6 -> x0, other arithmetic: 2.33 us -> none  [the longest x2 2.28 us: body(): return (eta[None], jnp.stack([mom_row, mom_col])[:, None])]
  transfers between devices with their start and end apart: 2 -> 0, of which waited for: 1 -> 0; matrix products, arithmetic and copies ran while one was open for 1% -> 0% of each run, Pallas kernels for 0% -> 0%
where the time goes in v1:
time: 22.9 us; the launch traced here: 22.7 us
  Pallas kernels  19.1 us (83%)
  local copies, waits for them, and re-layouts  2.95 us (13%)
  between operations  0.65 us (3%)
    pallas_call x1, Pallas kernels, body(): pl.pallas_call(functools.partial(kernel, patches, levels, rows, cols), ou...  19.1 us
    unnamed x4, local copies, waits for them, and re-layouts  2.95 us

profile of v1, /device:TPU:0, one launch (start us, length us, event | category | flops | bytes accessed | tf_op | source)
XLA Modules:
  0.0 22.7 jit_solution(7590609297048426628)
XLA Ops:
  0.6 19.1 %shard_map.86 = (f32[1,128,1024]{2,1,0:T(8,128)}, f32[2,1,128,1024]{3,2,1,0:T(8,128)}) custom-call(s32[1,4,4]{2,1,0:T(4,128)} %adj.1, f32[1,128,1024]{2,1,0:T(8,128)} %eta_hbm.1, f32[2,1,128,1024]{3,2,1,0:T(8,128)} %mom_hbm.1, f32[1,128,1024]{2,1,0:T(8,128)} %depth_hbm.1, s32[1,128,1024]{2,1,0:T(8,128)} %wet_hbm.1, f32[2,1024]{1,0:T(2,128)} %gain_hbm.1, ...), custom_call_target="tpu_custom_call" | custom-call | tf_op jit(solution)/shard_map/pallas_call | solution.py:305
  19.7 0.0 copy-start
  19.8 2.0 %copy.11 = f32[1,128,1024]{2,1,0:T(8,128)} copy(f32[1,128,1024]{2,1,0:T(8,128)} %get-tuple-element.4) | data formatting | bytes 1048576
  21.7 0.0 copy-done
  21.7 1.0 %copy.12 = f32[2,1,128,1024]{3,2,1,0:T(8,128)} copy(f32[2,1,128,1024]{3,2,1,0:T(8,128)S(1)} %copy-done) | data formatting | bytes 2097152
Async XLA Ops:
  19.7 2.0 %copy-start = (f32[2,1,128,1024]{3,2,1,0:T(8,128)S(1)}, f32[2,1,128,1024]{3,2,1,0:T(8,128)}, u32[]{:S(2)}) copy-start(f32[2,1,128,1024]{3,2,1,0:T(8,128)} %get-tuple-element.5) | copy-start | bytes 3145732

commit v2 on v1

--- a/solution.py
+++ b/solution.py
@@ -11,15 +11,59 @@
 COURANT = 0.45
 LANES = 128
 BLOCK = 8
-
-
-def kernel(patches, levels, rows, cols,
-           adj, eta_hbm, mom_hbm, depth_hbm, wet_hbm, gain_hbm, table_hbm,
-           eta_out, mom_out,
-           E, Pm, Q, H, W, gain_v, table_v, f8, idx8, gain8, tmp,
-           sfirst, slast, scol, sinf, sew,
-           rown, in_sems, out_sems, send_sems, recv_sems, own_sems, *landing):
+GROUP = 32
+
+
+def advance(r, E, Pm, Q, H, W, halo, E_to, P_to, Q_to):
+    cols = Pm.shape[1]
+    lane_ids = lax.broadcasted_iota(jnp.int32, (BLOCK, cols), 1)
+    span = slice(r, r + BLOCK)
+    e = E[span, :]
+    wet = W[span, :].astype(jnp.float32)
+    e_south = E[r + 1:r + 1 + BLOCK, :]
+    e_east = pltpu.roll(e, cols - 1, 1)
+    if halo is not None:
+        e_east = jnp.where(lane_ids == cols - 1, halo[span, 0:1], e_east)
+    p = wet * (Pm[span, :] - COURANT * (e_east - e))
+    q = wet * (Q[8 + r:16 + r, :] - COURANT * (e_south - e))
+    p_west = pltpu.roll(p, 1, 1)
+    if halo is not None:
+        p_edge = halo[span, 1:2] - COURANT * halo[span, 2:3] * e[:, 0:1]
+        p_west = jnp.where(lane_ids == 0, p_edge, p_west)
+    P_to[span, :] = p
+    Q_to[8 + r:16 + r, :] = q
+    q_north = Q_to[7 + r:15 + r, :]
+    E_to[span, :] = wet * (e - COURANT * H[span, :] * ((p - p_west) + (q - q_north)))
+
+
+def finish(rows, E, Pm, Q, H, W, halo, eta_out, mom_out, E2, P2, Q2, sems):
+    Q2[7:8, :] = Q[7:8, :]
+    stores = []
+    edges = halo[...]
+    for r in range(0, rows, BLOCK):
+        advance(r, E, Pm, Q, H, W, edges, E2, P2, Q2)
+        if (r + BLOCK) % GROUP == 0:
+            g = r // GROUP
+            at = slice(g * GROUP, (g + 1) * GROUP)
+            for n, (src, dst) in enumerate((
+                    (P2.at[at], mom_out.at[0, 0, at]),
+                    (Q2.at[8 + g * GROUP:8 + (g + 1) * GROUP], mom_out.at[1, 0, at]),
+                    (E2.at[at], eta_out.at[0, at]))):
+                store = pltpu.make_async_copy(src, dst, sems.at[g, n])
+                store.start()
+                stores.append(store)
+    for store in stores:
+        store.wait()
+
+
+def exchange(patches, levels, rows, cols,
+             adj, eta_hbm, mom_hbm, depth_hbm, wet_hbm, gain_hbm, table_hbm,
+             E1, P1, Q1, H, W, halo_out,
+             E0, P0, Q0, gain_v, table_v, f8, idx8, gain8, tmp,
+             sfirst, slast, scol, sinf, sew,
+             rown, in_sems, send_sems, recv_sems, own_sems, *landing):
     rfirst, rlast, rcol, rnbr, rew = (landing[n * STEPS:(n + 1) * STEPS] for n in range(5))
+    fields = ((E0, P0, Q0), (E1, P1, Q1))
     patch = lax.axis_index("patch")
     level = lax.axis_index("level")
     half = lax.axis_index("sub")
@@ -27,9 +71,9 @@
     other = 1 - half
 
     loads = [
-        pltpu.make_async_copy(eta_hbm.at[0], E.at[0:rows], in_sems.at[0]),
-        pltpu.make_async_copy(mom_hbm.at[0, 0], Pm, in_sems.at[1]),
-        pltpu.make_async_copy(mom_hbm.at[1, 0], Q.at[8:8 + rows], in_sems.at[2]),
+        pltpu.make_async_copy(eta_hbm.at[0], E0.at[0:rows], in_sems.at[0]),
+        pltpu.make_async_copy(mom_hbm.at[0, 0], P0, in_sems.at[1]),
+        pltpu.make_async_copy(mom_hbm.at[1, 0], Q0.at[8:8 + rows], in_sems.at[2]),
         pltpu.make_async_copy(wet_hbm.at[0], W, in_sems.at[3]),
         pltpu.make_async_copy(table_hbm, table_v, in_sems.at[4]),
         pltpu.make_async_copy(gain_hbm, gain_v, in_sems.at[5]),
@@ -61,9 +105,6 @@
         for d in range(patches):
             greet(d, half, level + 1)
             greet(d, other, level + 1)
-
-    sides = (level > 0).astype(jnp.int32) + (level < levels - 1).astype(jnp.int32)
-    pl.semaphore_wait(barrier, 2 * patches - 1 + 2 * patches * sides)
 
     for load in loads[:6]:
         load.wait()
@@ -109,7 +150,8 @@
             recv_sem=own_sems.at[t, 1], device_id={"level": lower},
             device_id_type=pl.DeviceIdType.MESH)
 
-    def send_inflow(t):
+    def make_inflow(t):
+        E = fields[t][0]
         for c in range(chunks):
             f8[c:c + 1, :] = E[0:1, c * LANES:(c + 1) * LANES]
         index = idx8[...]
@@ -122,9 +164,11 @@
             picked = jnp.where(which == c, got, picked)
         inflow = gain8[...] * picked
         sinf[t] = inflow
-        own_copy(t).start()
         sew[t, 0:1, :] = inflow[0:1, :]
         sew[t, 1:2, :] = pltpu.roll(inflow[chunks - 1:chunks, :], 1, 1)
+
+    def send_inflow(t):
+        own_copy(t).start()
         for d in range(patches):
             beside, ends = inf_copies(t, patch, d)
 
@@ -182,14 +226,15 @@
     finer = level < levels - 1
     lane_ids = lax.broadcasted_iota(jnp.int32, (rows, LANES), 1)
     first_lane = lax.broadcasted_iota(jnp.int32, (1, LANES), 1) == 0
-    wide_ids = lax.broadcasted_iota(jnp.int32, (BLOCK, cols), 1)
     tail = slice(cols - LANES, cols)
     end = rows - 1
 
-    for t in range(STEPS):
+    def make_messages(t):
+        E, Pm, Q = fields[t]
+
         @pl.when(level == levels - 1)
         def _():
-            send_inflow(t)
+            make_inflow(t)
 
         sfirst[t] = E[0:1, :]
         wet_row = W[end:rows, :].astype(jnp.float32)
@@ -202,7 +247,16 @@
                           jnp.where(lane_ids == 1, pltpu.roll(share, 2, 1),
                                     pltpu.roll(wet_tail, 3, 1)))
         scol[t] = jnp.transpose(mixed)[0:8, :]
+
+    def send_messages(t):
+        @pl.when(level == levels - 1)
+        def _():
+            send_inflow(t)
+
         each_halo(t, 1, 0, lambda copy: copy.start(), True)
+
+    def receive(t):
+        E, Pm, Q = fields[t]
 
         @pl.when(finer)
         def _():
@@ -214,6 +268,7 @@
         if levels > 2:
             @pl.when(jnp.logical_and(level > 0, level < levels - 1))
             def _():
+                make_inflow(t)
                 send_inflow(t)
 
         each_halo(t, 0, 1, lambda copy: copy.wait_recv(), False)
@@ -232,7 +287,6 @@
         tmp[0:1, :] = jnp.where(east >= 0, east_row, 0.0)
         tmp[1:2, :] = jnp.where(west >= 0, share, 0.0)
         tmp[2:3, :] = jnp.where(west >= 0, wet_w, 0.0)
-        halo = jnp.transpose(tmp[...])
         beside = rnbr[t][south_at]
         below = rfirst[t][south_at]
         for c in range(chunks):
@@ -241,40 +295,45 @@
             E[rows:rows + 1, lane] = jnp.where(south_ok, value, 0.0)
         share_n = rlast[t][north_at, 1 if t == 0 else 0]
         wet_n = rlast[0][north_at, 0]
-        Q[7:8, :] = jnp.where(north_ok, share_n - COURANT * wet_n * E[0:1, :], 0.0)
-        if t == 0:
-            loads[6].wait()
-
-        for r in range(0, rows, BLOCK):
-            span = slice(r, r + BLOCK)
-            e = E[span, :]
-            wet = W[span, :].astype(jnp.float32)
-            e_south = E[r + 1:r + 1 + BLOCK, :]
-            e_east = jnp.where(wide_ids == cols - 1, halo[span, 0:1], pltpu.roll(e, cols - 1, 1))
-            p = wet * (Pm[span, :] - COURANT * (e_east - e))
-            q = wet * (Q[8 + r:16 + r, :] - COURANT * (e_south - e))
-            p_edge = halo[span, 1:2] - COURANT * halo[span, 2:3] * e[:, 0:1]
-            p_west = jnp.where(wide_ids == 0, p_edge, pltpu.roll(p, 1, 1))
-            Pm[span, :] = p
-            Q[8 + r:16 + r, :] = q
-            q_north = Q[7 + r:15 + r, :]
-            E[span, :] = wet * (e - COURANT * H[span, :] * ((p - p_west) + (q - q_north)))
-
-    stores = [
-        pltpu.make_async_copy(E.at[0:rows], eta_out.at[0], out_sems.at[0]),
-        pltpu.make_async_copy(Pm, mom_out.at[0, 0], out_sems.at[1]),
-        pltpu.make_async_copy(Q.at[8:8 + rows], mom_out.at[1, 0], out_sems.at[2]),
-    ]
-    for store in stores:
-        store.start()
+        Q_to = Q1
+        Q_to[7:8, :] = jnp.where(north_ok, share_n - COURANT * wet_n * E[0:1, :], 0.0)
+        return jnp.transpose(tmp[...])
+
+    make_messages(0)
+    sides = (level > 0).astype(jnp.int32) + (level < levels - 1).astype(jnp.int32)
+    pl.semaphore_wait(barrier, 2 * patches - 1 + 2 * patches * sides)
+    send_messages(0)
+    loads[6].wait()
+    for r in range(0, rows - BLOCK, BLOCK):
+        advance(r, E0, P0, Q0, H, W, None, E1, P1, Q1)
+    halo = receive(0)
+    for r in (0, rows - BLOCK):
+        advance(r, E0, P0, Q0, H, W, None, E1, P1, Q1)
+    head = slice(0, LANES)
+    e = E0[0:rows, head]
+    wet = W[:, head].astype(jnp.float32)
+    p_edge = halo[:, 1:2] - COURANT * halo[:, 2:3] * e[:, 0:1]
+    across = Q1[8:8 + rows, head] - Q1[7:7 + rows, head]
+    fixed = wet * (e - COURANT * H[:, head] * ((P1[:, head] - p_edge) + across))
+    E1[0:rows, head] = jnp.where(lane_ids == 0, fixed, E1[0:rows, head])
+    e = E0[0:rows, tail]
+    wet = W[:, tail].astype(jnp.float32)
+    p = wet * (P0[:, tail] - COURANT * (halo[:, 0:1] - e))
+    p = jnp.where(lane_ids == LANES - 1, p, P1[:, tail])
+    P1[:, tail] = p
+    across = Q1[8:8 + rows, tail] - Q1[7:7 + rows, tail]
+    fixed = wet * (e - COURANT * H[:, tail] * ((p - pltpu.roll(p, 1, 1)) + across))
+    E1[0:rows, tail] = jnp.where(lane_ids == LANES - 1, fixed, E1[0:rows, tail])
+
+    make_messages(1)
+    send_messages(1)
+    halo_out[...] = receive(1)
     for t in range(STEPS):
         each_halo(t, 1, 0, lambda copy: copy.wait_send(), True)
 
         @pl.when(level > 0)
         def _():
             inflow_send_waits(t)
-    for store in stores:
-        store.wait()
 
 
 def body(mesh, adjoint_height, adjoint_momenta, depth, wet_mask, adjacency, nest_gain, nest_index):
@@ -284,33 +343,42 @@
     f32 = jnp.float32
     anywhere = pl.BlockSpec(memory_space=pl.ANY)
     v = pltpu.VMEM
+    dma = pltpu.SemaphoreType.DMA
     scratch = [
         v((rows + 8, cols), f32), v((rows, cols), f32), v((rows + 8, cols), f32),
-        v((rows, cols), f32), v((rows, cols), jnp.int32),
         v(nest_gain.shape, f32), v(nest_index.shape, jnp.int32),
         v((chunks, LANES), f32), v((chunks, LANES), jnp.int32), v((chunks, LANES), f32),
         v((8, LANES), f32),
         v((STEPS, 1, cols), f32), v((STEPS + 1, 1, cols), f32), v((STEPS, 8, LANES), f32),
         v((STEPS, chunks, LANES), f32), v((STEPS, 2, LANES), f32),
         v((STEPS, chunks, LANES), f32),
-        pltpu.SemaphoreType.DMA((7,)), pltpu.SemaphoreType.DMA((3,)),
-        pltpu.SemaphoreType.DMA((STEPS, 5, patches)), pltpu.SemaphoreType.DMA((STEPS, 5, patches)),
-        pltpu.SemaphoreType.DMA((STEPS, 2)),
+        dma((7,)), dma((STEPS, 5, patches)), dma((STEPS, 5, patches)), dma((STEPS, 2)),
     ]
     scratch += [v((patches, 1, cols), f32)] * STEPS
     scratch += [v((patches, 2 if t == 0 else 1, 1, cols), f32) for t in range(STEPS)]
     scratch += [v((patches, 8, LANES), f32)] * STEPS
     scratch += [v((patches, chunks, LANES), f32)] * STEPS
     scratch += [v((patches, 2, LANES), f32)] * STEPS
-    return pl.pallas_call(
-        functools.partial(kernel, patches, levels, rows, cols),
-        out_shape=(jax.ShapeDtypeStruct(adjoint_height.shape, f32),
-                   jax.ShapeDtypeStruct(adjoint_momenta.shape, f32)),
+    here = pl.BlockSpec(memory_space=pltpu.VMEM)
+    state = pl.pallas_call(
+        functools.partial(exchange, patches, levels, rows, cols),
+        out_shape=(v((rows + 8, cols), f32), v((rows, cols), f32), v((rows + 8, cols), f32),
+                   v((rows, cols), f32), v((rows, cols), jnp.int32), v((rows, 8), f32)),
         in_specs=[pl.BlockSpec(memory_space=pltpu.SMEM)] + [anywhere] * 6,
-        out_specs=(anywhere, anywhere),
+        out_specs=(here,) * 6,
         scratch_shapes=scratch,
         compiler_params=pltpu.CompilerParams(collective_id=0, has_side_effects=True),
     )(adjacency, adjoint_height, adjoint_momenta, depth, wet_mask, nest_gain, nest_index)
+    state = [pltpu.with_memory_space_constraint(x, pltpu.VMEM) for x in state]
+    return pl.pallas_call(
+        functools.partial(finish, rows),
+        out_shape=(jax.ShapeDtypeStruct(adjoint_height.shape, f32),
+                   jax.ShapeDtypeStruct(adjoint_momenta.shape, f32)),
+        in_specs=[here] * 6,
+        out_specs=(anywhere, anywhere),
+        scratch_shapes=[v((rows + 8, cols), f32), v((rows, cols), f32), v((rows + 8, cols), f32),
+                        dma((rows // GROUP, 3))],
+    )(*state)
 
 
 def solution(mesh):

time: 22.9 us -> 19.3 us (0.84)
  local copies, waits for them, and re-layouts: 2.95 us -> 0 us
  Pallas kernels: 19.1 us -> 18.5 us
    unnamed x4 -> x0, local copies, waits for them, and re-layouts: 2.95 us -> none
    pallas_call x1 -> x2, Pallas kernels: 19.1 us -> 18.5 us  [the longest x1 15.8 us: body(): pl.pallas_call(functools.partial(exchange, patches, levels, rows, cols),...]
where the time goes in v2:
time: 19.3 us; the launch traced here: 19.1 us
  Pallas kernels  18.5 us (96%)
  between operations  0.64 us (3%)
    pallas_call x1, Pallas kernels, body(): pl.pallas_call(functools.partial(exchange, patches, levels, rows, cols),...  15.8 us
    pallas_call x1, Pallas kernels, body(): pl.pallas_call(functools.partial(finish, rows), out_shape=(jax.ShapeDtype...  2.71 us

profile of v2, /device:TPU:0, one launch (start us, length us, event | category | flops | bytes accessed | tf_op | source)
XLA Modules:
  0.0 19.1 jit_solution(16758280426995425749)
XLA Ops:
  0.6 15.8 %shard_map.86 = (f32[136,1024]{1,0:T(8,128)S(1)}, f32[128,1024]{1,0:T(8,128)S(1)}, f32[136,1024]{1,0:T(8,128)S(1)}, f32[128,1024]{1,0:T(8,128)S(1)}, s32[128,1024]{1,0:T(8,128)S(1)}, /*index=5*/f32[128,8]{1,0:T(8,128)S(1)}) custom-call(s32[1,4,4]{2,1,0:T(4,128)} %adj.1, f32[1,128,1024]{2,1,0:T(8,128)} %eta_hbm.1, f32[2,1,128,1024]{3,2,1,0:T(8,128)} %mom_hbm.1, ...), custom_call_target="tpu_custom_call" | custom-call | tf_op jit(solution)/shard_map/pallas_call | solution.py:363
  16.4 2.7 %shard_map.87 = (f32[1,128,1024]{2,1,0:T(8,128)}, f32[2,1,128,1024]{3,2,1,0:T(8,128)}) custom-call(f32[136,1024]{1,0:T(8,128)S(1)} %get-tuple-element.8.E, f32[128,1024]{1,0:T(8,128)S(1)} %get-tuple-element.9.Pm, f32[136,1024]{1,0:T(8,128)S(1)} %get-tuple-element.10.Q, f32[128,1024]{1,0:T(8,128)S(1)} %get-tuple-element.11.H, ...), custom_call_target="tpu_custom_call" | custom-call | tf_op jit(solution)/shard_map/pallas_call | solution.py:373

commit v3 on v2

--- a/solution.py
+++ b/solution.py
@@ -11,7 +11,6 @@
 COURANT = 0.45
 LANES = 128
 BLOCK = 8
-GROUP = 32
 
 
 def advance(r, E, Pm, Q, H, W, halo, E_to, P_to, Q_to):
@@ -36,30 +35,60 @@
     E_to[span, :] = wet * (e - COURANT * H[span, :] * ((p - p_west) + (q - q_north)))
 
 
-def finish(rows, E, Pm, Q, H, W, halo, eta_out, mom_out, E2, P2, Q2, sems):
-    Q2[7:8, :] = Q[7:8, :]
+def finish(rows, E, Pm, Q, H, W, halo, E2, P2, Q2, eta_out, mom_out, Ef, Pf, Qf, sems):
+    cols = Pm.shape[1]
+    end = rows - BLOCK
+    mid = slice(BLOCK, end)
+    head, tail = slice(0, LANES), slice(cols - LANES, cols)
+    before, inner = slice(0, cols - LANES), slice(LANES, cols - LANES)
     stores = []
+
+    def store(src, dst):
+        copy = pltpu.make_async_copy(src, dst, sems.at[len(stores)])
+        copy.start()
+        stores.append(copy)
+
+    eta_to, row_to, col_to = eta_out.at[0], mom_out.at[0, 0], mom_out.at[1, 0]
+    store(Q2.at[BLOCK + 8:end + 8], col_to.at[mid])
+    store(P2.at[mid, before], row_to.at[mid, before])
+    store(E2.at[mid, inner], eta_to.at[mid, inner])
     edges = halo[...]
-    for r in range(0, rows, BLOCK):
-        advance(r, E, Pm, Q, H, W, edges, E2, P2, Q2)
-        if (r + BLOCK) % GROUP == 0:
-            g = r // GROUP
-            at = slice(g * GROUP, (g + 1) * GROUP)
-            for n, (src, dst) in enumerate((
-                    (P2.at[at], mom_out.at[0, 0, at]),
-                    (Q2.at[8 + g * GROUP:8 + (g + 1) * GROUP], mom_out.at[1, 0, at]),
-                    (E2.at[at], eta_out.at[0, at]))):
-                store = pltpu.make_async_copy(src, dst, sems.at[g, n])
-                store.start()
-                stores.append(store)
-    for store in stores:
-        store.wait()
+    lane_ids = lax.broadcasted_iota(jnp.int32, (end - BLOCK, LANES), 1)
+
+    across = Q2[BLOCK + 8:end + 8, head] - Q2[BLOCK + 7:end + 7, head]
+    e = E[mid, head]
+    wet = W[mid, head].astype(jnp.float32)
+    p_edge = edges[mid, 1:2] - COURANT * edges[mid, 2:3] * e[:, 0:1]
+    fixed = wet * (e - COURANT * H[mid, head] * ((P2[mid, head] - p_edge) + across))
+    Ef[mid, head] = jnp.where(lane_ids == 0, fixed, E2[mid, head])
+    store(Ef.at[mid, head], eta_to.at[mid, head])
+
+    across = Q2[BLOCK + 8:end + 8, tail] - Q2[BLOCK + 7:end + 7, tail]
+    e = E[mid, tail]
+    wet = W[mid, tail].astype(jnp.float32)
+    p = wet * (Pm[mid, tail] - COURANT * (edges[mid, 0:1] - e))
+    p = jnp.where(lane_ids == LANES - 1, p, P2[mid, tail])
+    Pf[mid, tail] = p
+    store(Pf.at[mid, tail], row_to.at[mid, tail])
+    fixed = wet * (e - COURANT * H[mid, tail] * ((p - pltpu.roll(p, 1, 1)) + across))
+    Ef[mid, tail] = jnp.where(lane_ids == LANES - 1, fixed, E2[mid, tail])
+    store(Ef.at[mid, tail], eta_to.at[mid, tail])
+
+    for r in (0, end):
+        Qf[7 + r:8 + r, :] = (Q if r == 0 else Q2)[7 + r:8 + r, :]
+        advance(r, E, Pm, Q, H, W, edges, Ef, Pf, Qf)
+        at = slice(r, r + BLOCK)
+        store(Pf.at[at], row_to.at[at])
+        store(Qf.at[8 + r:16 + r], col_to.at[at])
+        store(Ef.at[at], eta_to.at[at])
+    for copy in stores:
+        copy.wait()
 
 
 def exchange(patches, levels, rows, cols,
-             adj, eta_hbm, mom_hbm, depth_hbm, wet_hbm, gain_hbm, table_hbm,
-             E1, P1, Q1, H, W, halo_out,
-             E0, P0, Q0, gain_v, table_v, f8, idx8, gain8, tmp,
+             adj_hbm, eta_hbm, mom_hbm, depth_hbm, wet_hbm, gain_hbm, table_hbm,
+             E1, P1, Q1, H, W, halo_out, E2, P2, Q2,
+             adj, E0, P0, Q0, gain_v, table_v, f8, idx8, gain8, tmp,
              sfirst, slast, scol, sinf, sew,
              rown, in_sems, send_sems, recv_sems, own_sems, *landing):
     rfirst, rlast, rcol, rnbr, rew = (landing[n * STEPS:(n + 1) * STEPS] for n in range(5))
@@ -77,11 +106,9 @@
         pltpu.make_async_copy(wet_hbm.at[0], W, in_sems.at[3]),
         pltpu.make_async_copy(table_hbm, table_v, in_sems.at[4]),
         pltpu.make_async_copy(gain_hbm, gain_v, in_sems.at[5]),
-        pltpu.make_async_copy(depth_hbm.at[0], H, in_sems.at[6]),
+        pltpu.make_async_copy(adj_hbm, adj, in_sems.at[6]),
+        pltpu.make_async_copy(depth_hbm.at[0], H, in_sems.at[7]),
     ]
-    for load in loads:
-        load.start()
-
     barrier = pltpu.get_barrier_semaphore()
 
     def greet(d, h, lev):
@@ -89,10 +116,10 @@
             "patch": lax.rem(patch + d, patches), "sub": h, "level": lev},
             device_id_type=pl.DeviceIdType.MESH)
 
-    for d in range(patches):
+    for d in range(patches - 1, -1, -1):
+        greet(d, other, level)
         if d:
             greet(d, half, level)
-        greet(d, other, level)
 
     @pl.when(level > 0)
     def _():
@@ -106,7 +133,10 @@
             greet(d, half, level + 1)
             greet(d, other, level + 1)
 
-    for load in loads[:6]:
+    for load in loads:
+        load.start()
+
+    for load in loads[:7]:
         load.wait()
 
     lower = jnp.maximum(level - 1, 0)
@@ -303,7 +333,7 @@
     sides = (level > 0).astype(jnp.int32) + (level < levels - 1).astype(jnp.int32)
     pl.semaphore_wait(barrier, 2 * patches - 1 + 2 * patches * sides)
     send_messages(0)
-    loads[6].wait()
+    loads[7].wait()
     for r in range(0, rows - BLOCK, BLOCK):
         advance(r, E0, P0, Q0, H, W, None, E1, P1, Q1)
     halo = receive(0)
@@ -327,6 +357,8 @@
 
     make_messages(1)
     send_messages(1)
+    for r in range(0, rows - BLOCK, BLOCK):
+        advance(r, E1, P1, Q1, H, W, None, E2, P2, Q2)
     halo_out[...] = receive(1)
     for t in range(STEPS):
         each_halo(t, 1, 0, lambda copy: copy.wait_send(), True)
@@ -344,15 +376,17 @@
     anywhere = pl.BlockSpec(memory_space=pl.ANY)
     v = pltpu.VMEM
     dma = pltpu.SemaphoreType.DMA
+    whole = (v((rows + 8, cols), f32), v((rows, cols), f32), v((rows + 8, cols), f32))
     scratch = [
-        v((rows + 8, cols), f32), v((rows, cols), f32), v((rows + 8, cols), f32),
+        pltpu.SMEM(adjacency.shape, jnp.int32),
+        *whole,
         v(nest_gain.shape, f32), v(nest_index.shape, jnp.int32),
         v((chunks, LANES), f32), v((chunks, LANES), jnp.int32), v((chunks, LANES), f32),
         v((8, LANES), f32),
         v((STEPS, 1, cols), f32), v((STEPS + 1, 1, cols), f32), v((STEPS, 8, LANES), f32),
         v((STEPS, chunks, LANES), f32), v((STEPS, 2, LANES), f32),
         v((STEPS, chunks, LANES), f32),
-        dma((7,)), dma((STEPS, 5, patches)), dma((STEPS, 5, patches)), dma((STEPS, 2)),
+        dma((8,)), dma((STEPS, 5, patches)), dma((STEPS, 5, patches)), dma((STEPS, 2)),
     ]
     scratch += [v((patches, 1, cols), f32)] * STEPS
     scratch += [v((patches, 2 if t == 0 else 1, 1, cols), f32) for t in range(STEPS)]
@@ -362,22 +396,23 @@
     here = pl.BlockSpec(memory_space=pltpu.VMEM)
     state = pl.pallas_call(
         functools.partial(exchange, patches, levels, rows, cols),
-        out_shape=(v((rows + 8, cols), f32), v((rows, cols), f32), v((rows + 8, cols), f32),
-                   v((rows, cols), f32), v((rows, cols), jnp.int32), v((rows, 8), f32)),
-        in_specs=[pl.BlockSpec(memory_space=pltpu.SMEM)] + [anywhere] * 6,
-        out_specs=(here,) * 6,
+        out_shape=(*whole, v((rows, cols), f32), v((rows, cols), jnp.int32), v((rows, 8), f32), *whole),
+        in_specs=[anywhere] * 7,
+        out_specs=(here,) * 9,
         scratch_shapes=scratch,
-        compiler_params=pltpu.CompilerParams(collective_id=0, has_side_effects=True),
-    )(adjacency, adjoint_height, adjoint_momenta, depth, wet_mask, nest_gain, nest_index)
+        compiler_params=pltpu.CompilerParams(collective_id=0, has_side_effects=True,
+                                             vmem_limit_bytes=12 << 20),
+    )(*[pltpu.with_memory_space_constraint(x, pltpu.HBM) for x in (
+        adjacency, adjoint_height, adjoint_momenta, depth, wet_mask, nest_gain, nest_index)])
     state = [pltpu.with_memory_space_constraint(x, pltpu.VMEM) for x in state]
     return pl.pallas_call(
         functools.partial(finish, rows),
         out_shape=(jax.ShapeDtypeStruct(adjoint_height.shape, f32),
                    jax.ShapeDtypeStruct(adjoint_momenta.shape, f32)),
-        in_specs=[here] * 6,
+        in_specs=[here] * 9,
         out_specs=(anywhere, anywhere),
-        scratch_shapes=[v((rows + 8, cols), f32), v((rows, cols), f32), v((rows + 8, cols), f32),
-                        dma((rows // GROUP, 3))],
+        scratch_shapes=[*whole, dma((12,))],
+        compiler_params=pltpu.CompilerParams(vmem_limit_bytes=12 << 20),
     )(*state)
 
 

time: 19.3 us -> 17.1 us (0.89)
  Pallas kernels: 18.5 us -> 16.4 us
    pallas_call x1, Pallas kernels: 2.71 us -> 1.23 us  [body(): pl.pallas_call(functools.partial(finish, rows), out_shape=(jax.ShapeDtype...]
    pallas_call x1, Pallas kernels: 15.8 us -> 15.1 us  [body(): pl.pallas_call(functools.partial(exchange, patches, levels, rows, cols),...]
where the time goes in v3:
time: 17.1 us; the launch traced here: 17 us
  Pallas kernels  16.4 us (96%)
  between operations  0.64 us (4%)
    pallas_call x1, Pallas kernels, body(): pl.pallas_call(functools.partial(exchange, patches, levels, rows, cols),...  15.1 us
    pallas_call x1, Pallas kernels, body(): pl.pallas_call(functools.partial(finish, rows), out_shape=(jax.ShapeDtype...  1.23 us

profile of v3, /device:TPU:0, one launch (start us, length us, event | category | flops | bytes accessed | tf_op | source)
XLA Modules:
  0.0 17.0 jit_solution(956351366207339694)
XLA Ops:
  0.6 15.1 %shard_map.86 = (f32[136,1024]{1,0:T(8,128)S(1)}, f32[128,1024]{1,0:T(8,128)S(1)}, f32[136,1024]{1,0:T(8,128)S(1)}, f32[128,1024]{1,0:T(8,128)S(1)}, s32[128,102...) custom-call(s32[1,4,4]{2,1,0:T(4,128)} %adj_hbm.1, ...), custom_call_target="tpu_custom_call" | custom-call | tf_op jit(solution)/shard_map/pallas_call | solution.py:397
  15.8 1.2 %shard_map.87 = (f32[1,128,1024]{2,1,0:T(8,128)}, f32[2,1,128,1024]{3,2,1,0:T(8,128)}) custom-call(f32[136,1024]{1,0:T(8,128)S(1)} %get-tuple-element.11.E, f32[128,1024]{1,0:T(8,128)S(1)} %get-tuple-element.12.Pm, f32[136,1024]{1,0:T(8,128)S(1)} %get-tuple-element.13.Q, f32[128,1024]{1,0:T(8,128)S(1)} %get-tuple-element.14.H, ...), custom_call_target="tpu_custom_call" | custom-call | tf_op jit(solution)/shard_map/pallas_call | solution.py:408

commit v4 on v3

--- a/solution.py
+++ b/solution.py
@@ -111,9 +111,11 @@
     ]
     barrier = pltpu.get_barrier_semaphore()
 
+    peers = [patch] + [lax.rem(patch + d, patches) for d in range(1, patches)]
+
     def greet(d, h, lev):
         pl.semaphore_signal(barrier, inc=1, device_id={
-            "patch": lax.rem(patch + d, patches), "sub": h, "level": lev},
+            "patch": peers[d], "sub": h, "level": lev},
             device_id_type=pl.DeviceIdType.MESH)
 
     for d in range(patches - 1, -1, -1):
@@ -153,26 +155,37 @@
         return pltpu.make_async_remote_copy(
             src_ref=src, dst_ref=buf, send_sem=send_sems.at[t, kind, d],
             recv_sem=recv_sems.at[t, kind, slot],
-            device_id={"patch": lax.rem(patch + d, patches), "sub": h, "level": lev},
+            device_id={"patch": peers[d], "sub": h, "level": lev},
             device_id_type=pl.DeviceIdType.MESH)
-
-    def slot_of(d):
-        return lax.rem(patch + d, patches)
 
     def last_part(t):
         return slice(0, 2) if t == 0 else slice(t + 1, t + 2)
 
-    def halo_copies(t, slot, d):
-        col = remote(t, 0, scol.at[t], rcol[t].at[slot], slot, d, half, level)
-        first = remote(t, 1, sfirst.at[t], rfirst[t].at[slot], slot, d, other, level)
+    def column_copy(t, slot, d):
+        return remote(t, 0, scol.at[t, 0:3], rcol[t].at[slot, 0:3], slot, d, half, level)
+
+    def first_copy(t, slot, d):
+        return remote(t, 1, sfirst.at[t], rfirst[t].at[slot], slot, d, other, level)
+
+    def last_copy(t, slot, d):
         part = last_part(t)
-        last = remote(t, 2, slast.at[part], rlast[t].at[slot], slot, d, other, level)
-        return col, first, last
-
-    def inf_copies(t, slot, d):
-        beside = remote(t, 3, sinf.at[t], rnbr[t].at[slot], slot, d, other, lower)
-        ends = remote(t, 4, sew.at[t], rew[t].at[slot], slot, d, half, lower)
-        return beside, ends
+        return remote(t, 2, slast.at[part], rlast[t].at[slot], slot, d, other, level)
+
+    def beside_copy(t, slot, d):
+        return remote(t, 3, sinf.at[t], rnbr[t].at[slot], slot, d, other, lower)
+
+    def ends_copy(t, slot, d):
+        return remote(t, 4, sew.at[t], rew[t].at[slot], slot, d, half, lower)
+
+    def per_half(across, inside, act):
+        @pl.when(half == across)
+        def _():
+            for d in range(1, patches):
+                act(d)
+
+        @pl.when(half == inside)
+        def _():
+            act(0)
 
     def own_copy(t):
         return pltpu.make_async_remote_copy(
@@ -199,49 +212,57 @@
 
     def send_inflow(t):
         own_copy(t).start()
-        for d in range(patches):
-            beside, ends = inf_copies(t, patch, d)
-
-            @pl.when(half == (1 if d == 0 else 0))
-            def _():
-                beside.start()
-            if d:
-                ends.start()
+        per_half(0, 1, lambda d: beside_copy(t, patch, d).start())
+        for d in range(1, patches):
+            ends_copy(t, patch, d).start()
 
     def inflow_waits(t):
-        for d in range(patches):
-            beside, ends = inf_copies(t, slot_of(d), d)
-
-            @pl.when(half == (0 if d == 0 else 1))
-            def _():
-                beside.wait_recv()
-            if d:
-                ends.wait_recv()
+        per_half(1, 0, lambda d: beside_copy(t, peers[d], d).wait_recv())
+        for d in range(1, patches):
+            ends_copy(t, peers[d], d).wait_recv()
 
     def inflow_send_waits(t):
         own_copy(t).wait_send()
-        for d in range(patches):
-            beside, ends = inf_copies(t, patch, d)
-
-            @pl.when(half == (1 if d == 0 else 0))
-            def _():
-                beside.wait_send()
-            if d:
-                ends.wait_send()
-
-    def each_halo(t, first_when, last_when, act, sending):
-        for d in range(patches):
-            col, first, last = halo_copies(t, patch if sending else slot_of(d), d)
-
-            @pl.when(half == (first_when if d == 0 else 1 - first_when))
-            def _():
-                act(first)
-
-            @pl.when(half == (last_when if d == 0 else 1 - last_when))
-            def _():
-                act(last)
-            if d:
-                act(col)
+        per_half(0, 1, lambda d: beside_copy(t, patch, d).wait_send())
+        for d in range(1, patches):
+            ends_copy(t, patch, d).wait_send()
+
+    def send_halos(t, act):
+        send_rows(t, act)
+        send_columns(t, act)
+
+    def send_columns(t, act):
+        for d in range(1, patches):
+            act(column_copy(t, patch, d))
+
+    def send_rows(t, act):
+        @pl.when(half == 0)
+        def _():
+            for d in range(1, patches):
+                act(first_copy(t, patch, d))
+            act(last_copy(t, patch, 0))
+
+        @pl.when(half == 1)
+        def _():
+            for d in range(1, patches):
+                act(last_copy(t, patch, d))
+            act(first_copy(t, patch, 0))
+
+    def receive_halos(t):
+        @pl.when(half == 0)
+        def _():
+            first_copy(t, peers[0], 0).wait_recv()
+            for d in range(1, patches):
+                last_copy(t, peers[d], d).wait_recv()
+
+        @pl.when(half == 1)
+        def _():
+            last_copy(t, peers[0], 0).wait_recv()
+            for d in range(1, patches):
+                first_copy(t, peers[d], d).wait_recv()
+
+        for d in range(1, patches):
+            column_copy(t, peers[d], d).wait_recv()
 
     north = adj[0, patch, 0]
     south = adj[0, patch, 1]
@@ -260,30 +281,36 @@
     end = rows - 1
 
     def make_messages(t):
+        @pl.when(level == levels - 1)
+        def _():
+            make_inflow(t)
+
+        make_rows(t)
+        make_columns(t)
+
+    def make_rows(t):
         E, Pm, Q = fields[t]
-
-        @pl.when(level == levels - 1)
-        def _():
-            make_inflow(t)
-
         sfirst[t] = E[0:1, :]
         wet_row = W[end:rows, :].astype(jnp.float32)
         slast[t + 1] = wet_row * (Q[8 + end:8 + rows, :] + COURANT * E[end:rows, :])
         if t == 0:
             slast[0] = wet_row
+
+    def make_columns(t):
+        E, Pm, Q = fields[t]
         wet_tail = W[:, tail].astype(jnp.float32)
         share = wet_tail * (Pm[:, tail] + COURANT * E[0:rows, tail])
         mixed = jnp.where(lane_ids == 0, E[0:rows, 0:LANES],
                           jnp.where(lane_ids == 1, pltpu.roll(share, 2, 1),
                                     pltpu.roll(wet_tail, 3, 1)))
-        scol[t] = jnp.transpose(mixed)[0:8, :]
+        scol[t] = jnp.transpose(mixed[:, 0:8])
 
     def send_messages(t):
         @pl.when(level == levels - 1)
         def _():
             send_inflow(t)
 
-        each_halo(t, 1, 0, lambda copy: copy.start(), True)
+        send_halos(t, lambda copy: copy.start())
 
     def receive(t):
         E, Pm, Q = fields[t]
@@ -301,7 +328,7 @@
                 make_inflow(t)
                 send_inflow(t)
 
-        each_halo(t, 0, 1, lambda copy: copy.wait_recv(), False)
+        receive_halos(t)
 
         @pl.when(finer)
         def _():
@@ -355,13 +382,20 @@
     fixed = wet * (e - COURANT * H[:, tail] * ((p - pltpu.roll(p, 1, 1)) + across))
     E1[0:rows, tail] = jnp.where(lane_ids == LANES - 1, fixed, E1[0:rows, tail])
 
-    make_messages(1)
-    send_messages(1)
+    @pl.when(level == levels - 1)
+    def _():
+        make_inflow(1)
+        send_inflow(1)
+
+    make_rows(1)
+    send_rows(1, lambda copy: copy.start())
+    make_columns(1)
+    send_columns(1, lambda copy: copy.start())
     for r in range(0, rows - BLOCK, BLOCK):
         advance(r, E1, P1, Q1, H, W, None, E2, P2, Q2)
     halo_out[...] = receive(1)
     for t in range(STEPS):
-        each_halo(t, 1, 0, lambda copy: copy.wait_send(), True)
+        send_halos(t, lambda copy: copy.wait_send())
 
         @pl.when(level > 0)
         def _():

time: 17.1 us -> 17 us (level)
  Pallas kernels: 16.4 us -> 16.2 us
where the time goes in v4:
time: 17 us; the launch traced here: 16.9 us
  Pallas kernels  16.2 us (95%)
  between operations  0.64 us (4%)
    pallas_call x1, Pallas kernels, body(): pl.pallas_call(functools.partial(exchange, patches, levels, rows, cols),...  15 us
    pallas_call x1, Pallas kernels, body(): pl.pallas_call(functools.partial(finish, rows), out_shape=(jax.ShapeDtype...  1.23 us

profile of v4, /device:TPU:0, one launch (start us, length us, event | category | flops | bytes accessed | tf_op | source)
XLA Modules:
  0.0 16.9 jit_solution(3242403045067675009)
XLA Ops:
  0.6 15.0 %shard_map.86 = (f32[136,1024]{1,0:T(8,128)S(1)}, f32[128,1024]{1,0:T(8,128)S(1)}, f32[136,1024]{1,0:T(8,128)S(1)}, f32[128,1024]{1,0:T(8,128)S(1)}, s32[128,102...) custom-call(s32[1,4,4]{2,1,0:T(4,128)} %adj_hbm.1, ...), custom_call_target="tpu_custom_call" | custom-call | tf_op jit(solution)/shard_map/pallas_call | solution.py:431
  15.6 1.2 %shard_map.87 = (f32[1,128,1024]{2,1,0:T(8,128)}, f32[2,1,128,1024]{3,2,1,0:T(8,128)}) custom-call(f32[136,1024]{1,0:T(8,128)S(1)} %get-tuple-element.11.E, f32[128,1024]{1,0:T(8,128)S(1)} %get-tuple-element.12.Pm, f32[136,1024]{1,0:T(8,128)S(1)} %get-tuple-element.13.Q, f32[128,1024]{1,0:T(8,128)S(1)} %get-tuple-element.14.H, ...), custom_call_target="tpu_custom_call" | custom-call | tf_op jit(solution)/shard_map/pallas_call | solution.py:442
